TPU v7x, 32 devices: a whole 2x2x4 slice. The times are simulated.
32 devices in a mesh: comp: 4 (over y, core), gx: 2 (over x), gy: 4 (over z).
Axes of the slice: x: 2, y: 2, z: 4, core: 2. Of those that a mesh axis runs over, the one named last changes fastest.
Arguments:
- state: float32 [32, 32, 128, 128], P('comp', 'gx', 'gy'), may hold values from -4 to 4
- levels: int32 [32, 128], P('gx', 'gy'), may hold values from 0 to 128
- reaction: float32 [3, 8, 8], replicated, may hold values from -2 to 2
Outputs:
- new_state: float32 [32, 32, 128, 128], P('comp', 'gx', 'gy')
Inputs may be any that keep to these rules, and one draw needn't show every extreme that they name: `levels`: 0 marks a land column, 128 a column of full depth.
All inputs are finite; a program needn't handle non-finite values.
Results may differ from a plain program's by a relative error of at most 0.00018.
Values sent between devices are 32-bit elements; how exact they have to be, the bound alone decides.
No kernel may reach another device: no remote copies, remote signals or barrier semaphores. Data moves between devices by JAX's collectives and lax.ppermute only.
A program may use at most 64 MiB of HBM per device.

v0:
```python
import jax
import jax.numpy as jnp
from jax import lax
from jax.sharding import PartitionSpec as P

ITERS = 3
time_step = 0.25
lateral_mix = 0.05
vertical_mix = 0.1
pressure_scale = 0.05
thermal_coef = 1.0
haline_coef = 0.8
coriolis_mean = 0.5
coriolis_slope = 0.5


def padded_2(cells, sides, width):
    for axis, dim in sides:
        count = lax.axis_size(axis)
        head = lax.slice_in_dim(cells, 0, width, axis=dim)
        tail = lax.slice_in_dim(cells, cells.shape[dim] - width, cells.shape[dim], axis=dim)
        cells = jnp.concatenate(
            [
                lax.ppermute(tail, axis, [(i, (i + 1) % count) for i in range(count)]),
                cells,
                lax.ppermute(head, axis, [((i + 1) % count, i) for i in range(count)]),
            ],
            axis=dim,
        )
    return cells


def from_root(block, axis, source):
    block = jnp.where(lax.axis_index(axis) == source, block, jnp.zeros_like(block))
    return lax.psum(block, axis)


def along(padded, axis, shift):
    count_x = padded.shape[1] - 4
    count_y = padded.shape[2] - 4
    if axis == 1:
        return padded[:, 2 + shift : 2 + shift + count_x, 2 : 2 + count_y]
    return padded[:, 2 : 2 + count_x, 2 + shift : 2 + shift + count_y]


def centered(padded, axis):
    return (
        8.0 * (along(padded, axis, 1) - along(padded, axis, -1))
        - (along(padded, axis, 2) - along(padded, axis, -2))
    ) / 12.0


def smoothing(padded, axis):
    return (
        along(padded, axis, 2)
        + along(padded, axis, -2)
        - 4.0 * (along(padded, axis, 1) + along(padded, axis, -1))
        + 6.0 * along(padded, axis, 0)
    ) / 12.0


def transport(padded, east, north):
    return (
        east * centered(padded, 1)
        + jnp.abs(east) * smoothing(padded, 1)
        + north * centered(padded, 2)
        + jnp.abs(north) * smoothing(padded, 2)
    )


def lateral(padded):
    return (
        along(padded, 1, 1)
        + along(padded, 1, -1)
        + along(padded, 2, 1)
        + along(padded, 2, -1)
        - 4.0 * along(padded, 1, 0)
    )


def vertical(center):
    column = jnp.pad(center, ((0, 0), (0, 0), (0, 0), (1, 1)))
    return column[..., 2:] + column[..., :-2] - 2.0 * center


def dynamics_step(padded, mask, latitude, accumulate):
    center = padded[:, 2:-2, 2:-2]
    east = center[0]
    north = center[1]
    moving = padded[0:4]
    density = haline_coef * padded[3] - thermal_coef * padded[2]
    pressure = (pressure_scale * accumulate(density))[None]
    tendency = (
        lateral_mix * lateral(moving)
        + vertical_mix * vertical(center[0:4])
        - transport(moving, east, north)
    )
    rotation = (coriolis_mean + coriolis_slope * latitude)[None, :, None]
    push_east = tendency[0] + rotation * north - centered(pressure, 1)[0]
    push_north = tendency[1] - rotation * east - centered(pressure, 2)[0]
    tendency = jnp.stack([push_east, push_north, tendency[2], tendency[3]])
    advanced = center[0:4] + time_step * (1.5 * tendency - 0.5 * center[4:8])
    return jnp.concatenate([advanced * mask, tendency * mask])


def tracer_step(padded, velocity, mask, coupling):
    center = padded[:, 2:-2, 2:-2]
    growth = 2.0 * jax.nn.sigmoid(velocity[2])
    reacting = growth * jnp.einsum(
        "ij,jxyz->ixyz", coupling, center, precision=lax.Precision.HIGHEST
    )
    tendency = (
        lateral_mix * lateral(padded)
        + vertical_mix * vertical(center)
        + reacting
        - transport(padded, velocity[0], velocity[1])
    )
    return (center + time_step * tendency) * mask


def per_device(state, levels, reaction):
    cells_y = state.shape[2]
    depth_count = state.shape[3]
    slot = lax.axis_index("comp")
    row_first = lax.axis_index("gy") * cells_y
    total_rows = cells_y * lax.axis_size("gy")
    depth = lax.broadcasted_iota(jnp.int32, (1, 1, depth_count), 2)
    mask = (depth < levels[:, :, None]).astype(jnp.float32)
    lower = lax.broadcasted_iota(jnp.int32, (depth_count, depth_count), 0)
    higher = lax.broadcasted_iota(jnp.int32, (depth_count, depth_count), 1)
    summing = (lower <= higher).astype(jnp.float32)
    coupling = lax.dynamic_index_in_dim(reaction, jnp.maximum(slot - 1, 0), 0, keepdims=False)

    def accumulate(density):
        return jnp.dot(density, summing, precision=lax.Precision.HIGHEST)

    def global_rows(width):
        return row_first - width + lax.iota(jnp.int32, cells_y + 2 * width)

    def latitude(width):
        rows = global_rows(width)
        return 2.0 * rows.astype(jnp.float32) / float(total_rows - 1) - 1.0

    current = state * mask[None]
    for step in range(ITERS):
        extend_padded = padded_2(current, (("gx", 1), ("gy", 2)), 2)
        inside_rows = global_rows(2)
        region_latitude = latitude(0)

        def run_dynamics(operands):
            return dynamics_step(operands[0], operands[2], region_latitude, accumulate)

        def run_tracers(operands):
            return tracer_step(operands[0], operands[1], operands[2], coupling)

        current = lax.cond(
            slot == 0,
            run_dynamics,
            run_tracers,
            (
                extend_padded
                * ((inside_rows >= 0) & (inside_rows < total_rows)).astype(jnp.float32)[
                    None, None, :, None
                ],
                from_root(current[0:3], "comp", 0),
                mask,
            ),
        )
    return current


def solution(mesh):
    in_specs = (P("comp", "gx", "gy", None), P("gx", "gy"), P())
    out_specs = P("comp", "gx", "gy", None)
    return jax.shard_map(
        per_device, mesh=mesh, in_specs=in_specs, out_specs=out_specs, check_vma=False
    )
```

profile of v0, /device:TPU:1, one launch (start us, length us, event | category | flops | bytes accessed | tf_op | source)
XLA Modules:
  0.0 190.1 jit_solution(14269763152524657210)
XLA Ops:
  6.5 0.8 fusion.99
  7.4 1.9 %broadcast_multiply_fusion = f32[8,16,32,128]{3,2,1,0:T(8,128)S(1)} fusion(f32[8,16,32,128]{3,2,1,0:T(8,128)} %param.9, f32[16,32,128]{2,1,0:T(8,128)S(1)} %fusion.99), kind=kLoop, calls=%fused_computation.174 | loop fusion | flops 524288 | bytes 4456448 | tf_op jit(solution)/shard_map/mul | solution.py:144
  9.4 2.1 %collective-permute-start = (f32[8,2,32,128]{3,2,1,0:T(8,128)S(1)}, f32[8,2,32,128]{3,2,1,0:T(8,128)S(1)}, u32[]{:S(2)}, u32[]{:S(2)}) collective-permute-start(f32[8,2,32,128]{3,2,1,0:T(8,128)S(1)} %get-tuple-element.149), channel_id=1, source_target_pairs={{0,4},{4,0},{1,5},{5,1},{2,6},{6,2},{3,7},{7,3},{8,12},{12,8},{9,1... | collective-permute-start | bytes 786440 | tf_op jit(solution)/shard_map/ppermute | solution.py:24
  11.6 1.0 slice_select_fusion.2
  13.2 4.2 %collective-permute-done = f32[8,2,32,128]{3,2,1,0:T(8,128)S(1)} collective-permute-done((f32[8,2,32,128]{3,2,1,0:T(8,128)S(1)}, f32[8,2,32,128]{3,2,1,0:T(8,128)S(1)}, u32[]{:S(2)}, u32[]{:S(2)}) %collective-permute-start) | collective-permute-done | bytes 262176 | tf_op jit(solution)/shard_map/ppermute | solution.py:24
  17.5 5.7 %collective-permute-done.1 = f32[8,2,32,128]{3,2,1,0:T(8,128)S(1)} collective-permute-done((f32[8,2,32,128]{3,2,1,0:T(8,128)S(1)}, f32[8,2,32,128]{3,2,1,0:T(8,128)S(1)}, u32[]{:S(2)}, u32[]{:S(2)}) %collective-permute-start.1) | collective-permute-done | bytes 262176 | tf_op jit(solution)/shard_map/ppermute | solution.py:26
  23.3 1.3 collective-permute-start.2
  24.7 2.1 %collective-permute-start.3 = (f32[8,20,2,128]{3,2,1,0:T(2,128)S(1)}, f32[8,20,2,128]{3,2,1,0:T(2,128)}, u32[]{:S(2)}, u32[]{:S(2)}) collective-permute-start(f32[8,20,2,128]{3,2,1,0:T(2,128)S(1)} %get-tuple-element.144), channel_id=1, source_target_pairs={{1,0},{2,1},{3,2},{0,3},{5,4},{6,5},{7,6},{4,7},{9,8},{10,9},{11,1... | collective-permute-start | bytes 491528 | tf_op jit(solution)/shard_map/ppermute | solution.py:26
  26.8 3.1 %collective-permute-done.2 = f32[8,20,2,128]{3,2,1,0:T(2,128)S(1)} collective-permute-done((f32[8,20,2,128]{3,2,1,0:T(2,128)S(1)}, f32[8,20,2,128]{3,2,1,0:T(2,128)S(1)}, u32[]{:S(2)}, u32[]{:S(2)}) %collective-permute-start.2) | collective-permute-done | bytes 163872 | tf_op jit(solution)/shard_map/ppermute | solution.py:24
  29.8 0.7 copy-done.14
  30.5 3.3 %collective-permute-done.3 = f32[8,20,2,128]{3,2,1,0:T(2,128)} collective-permute-done((f32[8,20,2,128]{3,2,1,0:T(2,128)S(1)}, f32[8,20,2,128]{3,2,1,0:T(2,128)}, u32[]{:S(2)}, u32[]{:S(2)}) %collective-permute-start.3) | collective-permute-done | bytes 163872 | tf_op jit(solution)/shard_map/ppermute | solution.py:26
  33.8 2.3 %maximum_multiply_fusion = f32[8,20,36,128]{3,2,1,0:T(8,128)S(1)} fusion(f32[8,20,2,128]{3,2,1,0:T(2,128)} %collective-permute-done.3, f32[8,2,32,128]{3,2,1,0:T(8,128)} %copy-done.7, f32[8,16,32,128]{3,2,1,0:T(8,128)} %copy-done.2, f32[8,2,32,128]{3,2,1,0:T(8,128)} %copy-done.6, f32[8,20,2,128]{3,2,1,0:T(2,128)} %copy-done.14, f32[36]{0:T(128)S(1)} %and_convert_fusion), kind=kLoop, calls=%fused_computation.171 | loop fusion | flops 3686400 | bytes 5898384 | tf_op jit(solution)/shard_map/mul | solution.py:161
  36.1 12.0 %all-reduce.10.cloned.1.call-done = f32[3,16,32,128]{3,2,1,0:T(8,128)} async-done(((f32[3,16,32,128]{3,2,1,0:T(8,128)}), f32[3,16,32,128]{3,2,1,0:T(8,128)}) %all-reduce.10.cloned.1.call-update) | async-done | bytes 786448 | tf_op jit(solution)/shard_map/psum | solution.py:35
  48.1 9.7 %conditional.3 = (f32[8,16,32,128]{3,2,1,0:T(8,128)S(1)}) conditional(s32[]{:T(128)} %convert_element_type.41, (f32[8,20,36,128]{3,2,1,0:T(8,128)S(1)}, f32[3,16,32,128]{3,2,1,0:T(8,128)}, f32[8,8]{1,0:T(8,128)S(1)}, f32[16,32,128]{2,1,0:T(8,128)S(1)}) %tuple.23, (f32[8,20,36,128]{3,2,1,0:T(8,128)S(1)}, f32[32]{0:T(128)S(1)}, f32[128,128]{1,0:T(8,128)}, ...), branch_computations={%region_1.2_spmd, %region_2.3_spmd} | conditional | flops 155859008 | bytes 41029640 | solution.py:156
  48.1 1.3 multiply_bitcast_fusion.4
  49.4 1.7 copy.9
  51.2 6.1 %fusion.8 = f32[8,16,32,128]{3,0,2,1:T(8,128)S(1)} fusion(f32[8,16,32,128]{3,0,2,1:T(8,128)S(1)} %slice.573, f32[8,20,36,128]{3,0,2,1:T(8,128)S(1)} %copy.9, f32[16,32,128]{2,1,0:T(8,128)S(1)} %get-tuple-element.65, f32[16,32,128]{2,1,0:T(8,128)S(1)} %get-tuple-element.102, f32[16,32,128]{2,1,0:T(8,128)S(1)} %get-tuple-element.104, ...), kind=kOutput, calls=%fused_computation.10 | convolution fusion | flops 72351744 | bytes 24645632 | tf_op jit(solution)/shard_map/cond/branch_0_fun/ij,jxyz->ixyz/dot_general | solution.py:109
  57.9 1.7 collective-permute-start.4
  59.6 6.8 %collective-permute-done.4 = f32[8,2,32,128]{3,2,1,0:T(8,128)S(1)} collective-permute-done((f32[8,2,32,128]{3,2,1,0:T(8,128)S(1)}, f32[8,2,32,128]{3,2,1,0:T(8,128)S(1)}, u32[]{:S(2)}, u32[]{:S(2)}) %collective-permute-start.4) | collective-permute-done | bytes 262176 | tf_op jit(solution)/shard_map/ppermute | solution.py:24
  66.4 2.8 %collective-permute-done.5 = f32[8,2,32,128]{3,2,1,0:T(8,128)S(1)} collective-permute-done((f32[8,2,32,128]{3,2,1,0:T(8,128)S(1)}, f32[8,2,32,128]{3,2,1,0:T(8,128)S(1)}, u32[]{:S(2)}, u32[]{:S(2)}) %collective-permute-start.5) | collective-permute-done | bytes 262176 | tf_op jit(solution)/shard_map/ppermute | solution.py:26
  69.9 1.2 collective-permute-start.6
  71.1 2.1 %collective-permute-start.7 = (f32[8,20,2,128]{3,2,1,0:T(2,128)S(1)}, f32[8,20,2,128]{3,2,1,0:T(2,128)}, u32[]{:S(2)}, u32[]{:S(2)}) collective-permute-start(f32[8,20,2,128]{3,2,1,0:T(2,128)S(1)} %get-tuple-element.142), channel_id=1, source_target_pairs={{1,0},{2,1},{3,2},{0,3},{5,4},{6,5},{7,6},{4,7},{9,8},{10,9},{11,1... | collective-permute-start | bytes 491528 | tf_op jit(solution)/shard_map/ppermute | solution.py:26
  73.2 1.0 slice_select_fusion.1
  74.2 3.5 %collective-permute-done.6 = f32[8,20,2,128]{3,2,1,0:T(2,128)S(1)} collective-permute-done((f32[8,20,2,128]{3,2,1,0:T(2,128)S(1)}, f32[8,20,2,128]{3,2,1,0:T(2,128)S(1)}, u32[]{:S(2)}, u32[]{:S(2)}) %collective-permute-start.6) | collective-permute-done | bytes 163872 | tf_op jit(solution)/shard_map/ppermute | solution.py:24
  77.7 0.7 copy-done.12
  78.3 0.9 collective-permute-done.7
  79.3 2.3 %maximum_multiply_fusion.1 = f32[8,20,36,128]{3,2,1,0:T(8,128)S(1)} fusion(f32[8,20,2,128]{3,2,1,0:T(2,128)} %collective-permute-done.7, f32[8,2,32,128]{3,2,1,0:T(8,128)} %copy-done.10, f32[8,16,32,128]{3,2,1,0:T(8,128)} %copy-done.3, f32[8,2,32,128]{3,2,1,0:T(8,128)} %copy-done.8, f32[8,20,2,128]{3,2,1,0:T(2,128)} %copy-done.12, f32[36]{0:T(128)S(1)} %and_convert_fusion), kind=kLoop, calls=%fused_computation.172 | loop fusion | flops 3686400 | bytes 5898384 | tf_op jit(solution)/shard_map/mul | solution.py:161
  81.5 28.3 %all-reduce.12.cloned.1.call-done = f32[3,16,32,128]{3,2,1,0:T(8,128)} async-done(((f32[3,16,32,128]{3,2,1,0:T(8,128)}), f32[3,16,32,128]{3,2,1,0:T(8,128)}) %all-reduce.12.cloned.1.call-update) | async-done | bytes 786448 | tf_op jit(solution)/shard_map/psum | solution.py:35
  109.8 9.7 %conditional.4 = (f32[8,16,32,128]{3,2,1,0:T(8,128)S(1)}) conditional(s32[]{:T(128)} %convert_element_type.41, (f32[8,20,36,128]{3,2,1,0:T(8,128)S(1)}, f32[3,16,32,128]{3,2,1,0:T(8,128)}, f32[8,8]{1,0:T(8,128)S(1)}, f32[16,32,128]{2,1,0:T(8,128)S(1)}) %tuple.25, (f32[8,20,36,128]{3,2,1,0:T(8,128)S(1)}, f32[32]{0:T(128)S(1)}, f32[128,128]{1,0:T(8,128)}, ...), branch_computations={%region_4.5_spmd, %region_5.6_spmd} | conditional | flops 155859008 | bytes 41029640 | solution.py:156
  109.8 1.3 multiply_bitcast_fusion.13
  111.1 1.7 copy.10
  113.0 6.1 %fusion.41 = f32[8,16,32,128]{3,0,2,1:T(8,128)S(1)} fusion(f32[8,16,32,128]{3,0,2,1:T(8,128)S(1)} %slice.593, f32[8,20,36,128]{3,0,2,1:T(8,128)S(1)} %copy.10, f32[16,32,128]{2,1,0:T(8,128)S(1)} %get-tuple-element.73, f32[16,32,128]{2,1,0:T(8,128)S(1)} %get-tuple-element.115, f32[16,32,128]{2,1,0:T(8,128)S(1)} %get-tuple-element.117, ...), kind=kOutput, calls=%fused_computation.67 | convolution fusion | flops 72351744 | bytes 24645632 | tf_op jit(solution)/shard_map/cond/branch_0_fun/ij,jxyz->ixyz/dot_general | solution.py:109
  119.6 1.7 collective-permute-start.8
  121.4 6.8 %collective-permute-done.8 = f32[8,2,32,128]{3,2,1,0:T(8,128)S(1)} collective-permute-done((f32[8,2,32,128]{3,2,1,0:T(8,128)S(1)}, f32[8,2,32,128]{3,2,1,0:T(8,128)S(1)}, u32[]{:S(2)}, u32[]{:S(2)}) %collective-permute-start.8) | collective-permute-done | bytes 262176 | tf_op jit(solution)/shard_map/ppermute | solution.py:24
  128.2 2.8 %collective-permute-done.9 = f32[8,2,32,128]{3,2,1,0:T(8,128)S(1)} collective-permute-done((f32[8,2,32,128]{3,2,1,0:T(8,128)S(1)}, f32[8,2,32,128]{3,2,1,0:T(8,128)S(1)}, u32[]{:S(2)}, u32[]{:S(2)}) %collective-permute-start.9) | collective-permute-done | bytes 262176 | tf_op jit(solution)/shard_map/ppermute | solution.py:26
  131.7 1.2 collective-permute-start.10
  132.9 2.1 %collective-permute-start.11 = (f32[8,20,2,128]{3,2,1,0:T(2,128)S(1)}, f32[8,20,2,128]{3,2,1,0:T(2,128)}, u32[]{:S(2)}, u32[]{:S(2)}) collective-permute-start(f32[8,20,2,128]{3,2,1,0:T(2,128)S(1)} %get-tuple-element.140), channel_id=1, source_target_pairs={{1,0},{2,1},{3,2},{0,3},{5,4},{6,5},{7,6},{4,7},{9,8},{10,9},{11,1... | collective-permute-start | bytes 491528 | tf_op jit(solution)/shard_map/ppermute | solution.py:26
  134.9 1.0 slice_select_fusion
  135.9 3.5 %collective-permute-done.10 = f32[8,20,2,128]{3,2,1,0:T(2,128)S(1)} collective-permute-done((f32[8,20,2,128]{3,2,1,0:T(2,128)S(1)}, f32[8,20,2,128]{3,2,1,0:T(2,128)S(1)}, u32[]{:S(2)}, u32[]{:S(2)}) %collective-permute-start.10) | collective-permute-done | bytes 163872 | tf_op jit(solution)/shard_map/ppermute | solution.py:24
  140.1 0.9 collective-permute-done.11
  141.0 2.3 %maximum_multiply_fusion.2 = f32[8,20,36,128]{3,2,1,0:T(8,128)S(1)} fusion(f32[8,20,2,128]{3,2,1,0:T(2,128)} %collective-permute-done.11, f32[8,2,32,128]{3,2,1,0:T(8,128)} %copy-done.11, f32[8,16,32,128]{3,2,1,0:T(8,128)} %copy-done.4, f32[8,2,32,128]{3,2,1,0:T(8,128)} %copy-done.9, f32[8,20,2,128]{3,2,1,0:T(2,128)} %copy-done.13, f32[36]{0:T(128)S(1)} %and_convert_fusion), kind=kLoop, calls=%fused_computation.173 | loop fusion | flops 3686400 | bytes 5898384 | tf_op jit(solution)/shard_map/mul | solution.py:161
  143.3 28.3 %all-reduce.14.cloned.1.call-done = f32[3,16,32,128]{3,2,1,0:T(8,128)} async-done(((f32[3,16,32,128]{3,2,1,0:T(8,128)}), f32[3,16,32,128]{3,2,1,0:T(8,128)}) %all-reduce.14.cloned.1.call-update) | async-done | bytes 786448 | tf_op jit(solution)/shard_map/psum | solution.py:35
  171.6 9.9 %conditional.5 = (f32[8,16,32,128]{3,2,1,0:T(8,128)S(1)}) conditional(s32[]{:T(128)} %convert_element_type.41, (f32[8,20,36,128]{3,2,1,0:T(8,128)S(1)}, f32[3,16,32,128]{3,2,1,0:T(8,128)}, f32[8,8]{1,0:T(8,128)S(1)}, f32[16,32,128]{2,1,0:T(8,128)S(1)}) %tuple.27, (f32[8,20,36,128]{3,2,1,0:T(8,128)S(1)}, f32[32]{0:T(128)S(1)}, f32[128,128]{1,0:T(8,128)}, ...), branch_computations={%region_7.8_spmd, %region_8.9_spmd} | conditional | flops 155859008 | bytes 41029640 | solution.py:156
  171.6 1.3 multiply_bitcast_fusion.22
  172.9 1.7 copy.11
  174.8 6.1 %fusion.74 = f32[8,16,32,128]{3,0,2,1:T(8,128)S(1)} fusion(f32[8,16,32,128]{3,0,2,1:T(8,128)S(1)} %slice.613, f32[8,20,36,128]{3,0,2,1:T(8,128)S(1)} %copy.11, f32[16,32,128]{2,1,0:T(8,128)S(1)} %get-tuple-element.81, f32[16,32,128]{2,1,0:T(8,128)S(1)} %get-tuple-element.128, f32[16,32,128]{2,1,0:T(8,128)S(1)} %get-tuple-element.130, ...), kind=kOutput, calls=%fused_computation.124 | convolution fusion | flops 72351744 | bytes 24645632 | tf_op jit(solution)/shard_map/cond/branch_0_fun/ij,jxyz->ixyz/dot_general | solution.py:109
  181.5 1.3 copy-done.5
  182.9 0.7 copy-done.1
  (51 shorter events, 5.0 us)
Async XLA Ops:
  6.5 6.1 %copy-start = (f32[3,8,8]{2,1,0:T(8,128)S(1)}, f32[3,8,8]{2,1,0:T(8,128)}, u32[]{:S(2)}) copy-start(f32[3,8,8]{2,1,0:T(8,128)} %param.11) | copy-start | bytes 2308
  6.5 41.6 %all-reduce.10.cloned.1.call-start = ((), (), s32[]{:S(2)}) async-start(), calls=%async_computation | async-start | bytes 1572864 | tf_op jit(solution)/shard_map/psum | solution.py:35
  9.3 14.0 %copy-start.2 = (f32[8,16,32,128]{3,2,1,0:T(8,128)}, f32[8,16,32,128]{3,2,1,0:T(8,128)S(1)}, u32[]{:S(2)}) copy-start(f32[8,16,32,128]{3,2,1,0:T(8,128)S(1)} %broadcast_multiply_fusion) | copy-start | bytes 6291460
  9.4 8.1 %collective-permute-start = (f32[8,2,32,128]{3,2,1,0:T(8,128)S(1)}, f32[8,2,32,128]{3,2,1,0:T(8,128)S(1)}, u32[]{:S(2)}, u32[]{:S(2)}) collective-permute-start(f32[8,2,32,128]{3,2,1,0:T(8,128)S(1)} %get-tuple-element.149), channel_id=1, source_target_pairs={{0,4},{4,0},{1,5},{5,1},{2,6},{6,2},{3,7},{7,3},{8,12},{12,8},{9,1... | collective-permute-start | bytes 786440 | tf_op jit(solution)/shard_map/ppermute | solution.py:24
  11.5 11.7 %collective-permute-start.1 = (f32[8,2,32,128]{3,2,1,0:T(8,128)S(1)}, f32[8,2,32,128]{3,2,1,0:T(8,128)S(1)}, u32[]{:S(2)}, u32[]{:S(2)}) collective-permute-start(f32[8,2,32,128]{3,2,1,0:T(8,128)S(1)} %get-tuple-element.150), channel_id=1, source_target_pairs={{4,0},{0,4},{5,1},{1,5},{6,2},{2,6},{7,3},{3,7},{12,8},{8,12},{13,... | collective-permute-start | bytes 786440 | tf_op jit(solution)/shard_map/ppermute | solution.py:26
  12.5 97.3 %all-reduce.12.cloned.1.call-start = ((), (), s32[]{:S(2)}) async-start(), calls=%async_computation.1 | async-start | bytes 1572864 | tf_op jit(solution)/shard_map/psum | solution.py:35
  17.5 12.4 %copy-start.6 = (f32[8,2,32,128]{3,2,1,0:T(8,128)}, f32[8,2,32,128]{3,2,1,0:T(8,128)S(1)}, u32[]{:S(2)}) copy-start(f32[8,2,32,128]{3,2,1,0:T(8,128)S(1)} %collective-permute-done) | copy-start | bytes 786436
  23.2 6.6 %copy-start.7 = (f32[8,2,32,128]{3,2,1,0:T(8,128)}, f32[8,2,32,128]{3,2,1,0:T(8,128)S(1)}, u32[]{:S(2)}) copy-start(f32[8,2,32,128]{3,2,1,0:T(8,128)S(1)} %collective-permute-done.1) | copy-start | bytes 786436
  23.3 6.5 %collective-permute-start.2 = (f32[8,20,2,128]{3,2,1,0:T(2,128)S(1)}, f32[8,20,2,128]{3,2,1,0:T(2,128)S(1)}, u32[]{:S(2)}, u32[]{:S(2)}) collective-permute-start(f32[8,20,2,128]{3,2,1,0:T(2,128)S(1)} %get-tuple-element.143), channel_id=1, source_target_pairs={{0,1},{1,2},{2,3},{3,0},{4,5},{5,6},{6,7},{7,4},{8,9},{9,10},{10,1... | collective-permute-start | bytes 491528 | tf_op jit(solution)/shard_map/ppermute | solution.py:24
  24.7 9.2 %collective-permute-start.3 = (f32[8,20,2,128]{3,2,1,0:T(2,128)S(1)}, f32[8,20,2,128]{3,2,1,0:T(2,128)}, u32[]{:S(2)}, u32[]{:S(2)}) collective-permute-start(f32[8,20,2,128]{3,2,1,0:T(2,128)S(1)} %get-tuple-element.144), channel_id=1, source_target_pairs={{1,0},{2,1},{3,2},{0,3},{5,4},{6,5},{7,6},{4,7},{9,8},{10,9},{11,1... | collective-permute-start | bytes 491528 | tf_op jit(solution)/shard_map/ppermute | solution.py:26
  29.8 0.7 copy-start.14
  57.8 16.3 %copy-start.3 = (f32[8,16,32,128]{3,2,1,0:T(8,128)}, f32[8,16,32,128]{3,2,1,0:T(8,128)S(1)}, u32[]{:S(2)}) copy-start(f32[8,16,32,128]{3,2,1,0:T(8,128)S(1)} %get-tuple-element.153) | copy-start | bytes 6291460
  57.9 8.5 %collective-permute-start.4 = (f32[8,2,32,128]{3,2,1,0:T(8,128)S(1)}, f32[8,2,32,128]{3,2,1,0:T(8,128)S(1)}, u32[]{:S(2)}, u32[]{:S(2)}) collective-permute-start(f32[8,2,32,128]{3,2,1,0:T(8,128)S(1)} %get-tuple-element.147), channel_id=1, source_target_pairs={{0,4},{4,0},{1,5},{5,1},{2,6},{6,2},{3,7},{7,3},{8,12},{12,8},{9,1... | collective-permute-start | bytes 786440 | tf_op jit(solution)/shard_map/ppermute | solution.py:24
  59.5 9.6 %collective-permute-start.5 = (f32[8,2,32,128]{3,2,1,0:T(8,128)S(1)}, f32[8,2,32,128]{3,2,1,0:T(8,128)S(1)}, u32[]{:S(2)}, u32[]{:S(2)}) collective-permute-start(f32[8,2,32,128]{3,2,1,0:T(8,128)S(1)} %get-tuple-element.148), channel_id=1, source_target_pairs={{4,0},{0,4},{5,1},{1,5},{6,2},{2,6},{7,3},{3,7},{12,8},{8,12},{13,... | collective-permute-start | bytes 786440 | tf_op jit(solution)/shard_map/ppermute | solution.py:26
  66.4 2.8 %copy-start.8 = (f32[8,2,32,128]{3,2,1,0:T(8,128)}, f32[8,2,32,128]{3,2,1,0:T(8,128)S(1)}, u32[]{:S(2)}) copy-start(f32[8,2,32,128]{3,2,1,0:T(8,128)S(1)} %collective-permute-done.4) | copy-start | bytes 786436
  69.2 0.7 copy-start.10
  69.9 7.8 %collective-permute-start.6 = (f32[8,20,2,128]{3,2,1,0:T(2,128)S(1)}, f32[8,20,2,128]{3,2,1,0:T(2,128)S(1)}, u32[]{:S(2)}, u32[]{:S(2)}) collective-permute-start(f32[8,20,2,128]{3,2,1,0:T(2,128)S(1)} %get-tuple-element.141), channel_id=1, source_target_pairs={{0,1},{1,2},{2,3},{3,0},{4,5},{5,6},{6,7},{7,4},{8,9},{9,10},{10,1... | collective-permute-start | bytes 491528 | tf_op jit(solution)/shard_map/ppermute | solution.py:24
  71.1 8.2 %collective-permute-start.7 = (f32[8,20,2,128]{3,2,1,0:T(2,128)S(1)}, f32[8,20,2,128]{3,2,1,0:T(2,128)}, u32[]{:S(2)}, u32[]{:S(2)}) collective-permute-start(f32[8,20,2,128]{3,2,1,0:T(2,128)S(1)} %get-tuple-element.142), channel_id=1, source_target_pairs={{1,0},{2,1},{3,2},{0,3},{5,4},{6,5},{7,6},{4,7},{9,8},{10,9},{11,1... | collective-permute-start | bytes 491528 | tf_op jit(solution)/shard_map/ppermute | solution.py:26
  74.2 97.4 %all-reduce.14.cloned.1.call-start = ((), (), s32[]{:S(2)}) async-start(), calls=%async_computation.2 | async-start | bytes 1572864 | tf_op jit(solution)/shard_map/psum | solution.py:35
  77.7 0.7 copy-start.12
  119.6 16.3 %copy-start.4 = (f32[8,16,32,128]{3,2,1,0:T(8,128)}, f32[8,16,32,128]{3,2,1,0:T(8,128)S(1)}, u32[]{:S(2)}) copy-start(f32[8,16,32,128]{3,2,1,0:T(8,128)S(1)} %get-tuple-element.154) | copy-start | bytes 6291460
  119.6 8.5 %collective-permute-start.8 = (f32[8,2,32,128]{3,2,1,0:T(8,128)S(1)}, f32[8,2,32,128]{3,2,1,0:T(8,128)S(1)}, u32[]{:S(2)}, u32[]{:S(2)}) collective-permute-start(f32[8,2,32,128]{3,2,1,0:T(8,128)S(1)} %get-tuple-element.145), channel_id=1, source_target_pairs={{0,4},{4,0},{1,5},{5,1},{2,6},{6,2},{3,7},{7,3},{8,12},{12,8},{9,1... | collective-permute-start | bytes 786440 | tf_op jit(solution)/shard_map/ppermute | solution.py:24
  121.3 9.6 %collective-permute-start.9 = (f32[8,2,32,128]{3,2,1,0:T(8,128)S(1)}, f32[8,2,32,128]{3,2,1,0:T(8,128)S(1)}, u32[]{:S(2)}, u32[]{:S(2)}) collective-permute-start(f32[8,2,32,128]{3,2,1,0:T(8,128)S(1)} %get-tuple-element.146), channel_id=1, source_target_pairs={{4,0},{0,4},{5,1},{1,5},{6,2},{2,6},{7,3},{3,7},{12,8},{8,12},{13,... | collective-permute-start | bytes 786440 | tf_op jit(solution)/shard_map/ppermute | solution.py:26
  128.2 2.8 %copy-start.9 = (f32[8,2,32,128]{3,2,1,0:T(8,128)}, f32[8,2,32,128]{3,2,1,0:T(8,128)S(1)}, u32[]{:S(2)}) copy-start(f32[8,2,32,128]{3,2,1,0:T(8,128)S(1)} %collective-permute-done.8) | copy-start | bytes 786436
  130.9 0.7 copy-start.11
  131.7 7.8 %collective-permute-start.10 = (f32[8,20,2,128]{3,2,1,0:T(2,128)S(1)}, f32[8,20,2,128]{3,2,1,0:T(2,128)S(1)}, u32[]{:S(2)}, u32[]{:S(2)}) collective-permute-start(f32[8,20,2,128]{3,2,1,0:T(2,128)S(1)} %get-tuple-element.139), channel_id=1, source_target_pairs={{0,1},{1,2},{2,3},{3,0},{4,5},{5,6},{6,7},{7,4},{8,9},{9,10},{10,1... | collective-permute-start | bytes 491528 | tf_op jit(solution)/shard_map/ppermute | solution.py:24
  132.9 8.2 %collective-permute-start.11 = (f32[8,20,2,128]{3,2,1,0:T(2,128)S(1)}, f32[8,20,2,128]{3,2,1,0:T(2,128)}, u32[]{:S(2)}, u32[]{:S(2)}) collective-permute-start(f32[8,20,2,128]{3,2,1,0:T(2,128)S(1)} %get-tuple-element.140), channel_id=1, source_target_pairs={{1,0},{2,1},{3,2},{0,3},{5,4},{6,5},{7,6},{4,7},{9,8},{10,9},{11,1... | collective-permute-start | bytes 491528 | tf_op jit(solution)/shard_map/ppermute | solution.py:26
  139.4 0.7 copy-start.13
  181.5 1.3 copy-start.5
  182.9 0.7 copy-start.1
Sparse Core Ops, SparseCore 0:
  12.7 35.3 all-reduce.9
  74.3 35.5 all-reduce.11
  136.0 35.5 all-reduce.13
where the time goes:
time: 191 us; the launch traced here: 190 us
  waiting for transfers between devices  113 us (59%)
  matrix products  18.4 us (10%)
  other arithmetic  17.3 us (9%)
  starting transfers between devices  15.7 us (8%)
  between operations  13.3 us (7%)
  local copies, waits for them, and re-layouts  12.1 us (6%)
    psum x3, waiting for transfers between devices, from_root(): return lax.psum(block, axis)  68.6 us
    ppermute x6, waiting for transfers between devices, padded_2(): lax.ppermute(tail, axis, [(i, (i + 1) % count) for i in range(count)])  27.8 us
    dot_general x3, matrix products, tracer_step(): jnp.einsum('ij,jxyz->ixyz', coupling, center, precision=lax.Precision.HIG...  18.4 us
    ppermute x6, waiting for transfers between devices, padded_2(): lax.ppermute(head, axis, [((i + 1) % count, i) for i in range(count)])  16.5 us
    ppermute x6, starting transfers between devices, padded_2(): lax.ppermute(tail, axis, [(i, (i + 1) % count) for i in range(count)])  9.18 us
    mul x3, other arithmetic, per_device(): extend_padded * ((inside_rows >= 0) & (inside_rows < total_rows)).astype(...  6.8 us
    ppermute x6, starting transfers between devices, padded_2(): lax.ppermute(head, axis, [((i + 1) % count, i) for i in range(count)])  6.44 us
    unnamed x30, local copies, waits for them, and re-layouts  5.23 us
  transfers between devices with their start and end apart: 15, of which 15 were waited for; matrix products, arithmetic and copies ran while one was open for 5% of the time, Pallas kernels for 0%

commit v1 on v0

--- a/solution.py
+++ b/solution.py
@@ -32,7 +32,7 @@
 
 def from_root(block, axis, source):
     block = jnp.where(lax.axis_index(axis) == source, block, jnp.zeros_like(block))
-    return lax.psum(block, axis)
+    return jnp.sum(lax.all_gather(block, axis_name=axis), axis=0)
 
 
 def along(padded, axis, shift):

time: 191 us -> 149 us (0.78)
  waiting for transfers between devices: 113 us -> 64.1 us
  other arithmetic: 17.3 us -> 27.4 us
  local copies, waits for them, and re-layouts: 12.1 us -> 9.62 us
    psum x3 -> x0, waiting for transfers between devices: 68.6 us -> none  [from_root(): return lax.psum(block, axis)]
    all_gather x0 -> x3, waiting for transfers between devices: none -> 25 us  [from_root(): return jnp.sum(lax.all_gather(block, axis_name=axis), axis=0)]
    reduce_sum x0 -> x3, other arithmetic: none -> 9.59 us  [from_root(): return jnp.sum(lax.all_gather(block, axis_name=axis), axis=0)]
    ppermute x6, waiting for transfers between devices: 27.8 us -> 21 us  [padded_2(): lax.ppermute(tail, axis, [(i, (i + 1) % count) for i in range(count)])]
    unnamed x30 -> x20, local copies, waits for them, and re-layouts: 5.23 us -> 2.72 us
  transfers between devices with their start and end apart: 15 -> 15, of which waited for: 15 -> 15; matrix products, arithmetic and copies ran while one was open for 5% -> 6% of each run, Pallas kernels for 0% -> 0%
where the time goes in v1:
time: 149 us; the launch traced here: 148 us
  waiting for transfers between devices  64.1 us (43%)
  other arithmetic  27.4 us (18%)
  matrix products  18.4 us (12%)
  starting transfers between devices  15.4 us (10%)
  between operations  13.3 us (9%)
  local copies, waits for them, and re-layouts  9.62 us (6%)
    all_gather x3, waiting for transfers between devices, from_root(): return jnp.sum(lax.all_gather(block, axis_name=axis), axis=0)  25 us
    ppermute x6, waiting for transfers between devices, padded_2(): lax.ppermute(tail, axis, [(i, (i + 1) % count) for i in range(count)])  21 us
    dot_general x3, matrix products, tracer_step(): jnp.einsum('ij,jxyz->ixyz', coupling, center, precision=lax.Precision.HIG...  18.4 us
    ppermute x6, waiting for transfers between devices, padded_2(): lax.ppermute(head, axis, [((i + 1) % count, i) for i in range(count)])  18.2 us
    reduce_sum x3, other arithmetic, from_root(): return jnp.sum(lax.all_gather(block, axis_name=axis), axis=0)  9.59 us
    ppermute x6, starting transfers between devices, padded_2(): lax.ppermute(tail, axis, [(i, (i + 1) % count) for i in range(count)])  8.43 us
    ppermute x6, starting transfers between devices, padded_2(): lax.ppermute(head, axis, [((i + 1) % count, i) for i in range(count)])  6.84 us
    mul x3, other arithmetic, per_device(): extend_padded * ((inside_rows >= 0) & (inside_rows < total_rows)).astype(...  6.57 us
  transfers between devices with their start and end apart: 15, of which 15 were waited for; matrix products, arithmetic and copies ran while one was open for 6% of the time, Pallas kernels for 0%

profile of v1, /device:TPU:1, one launch (start us, length us, event | category | flops | bytes accessed | tf_op | source)
XLA Modules:
  0.0 148.5 jit_solution(1359476267366360716)
XLA Ops:
  6.5 0.8 fusion.114
  7.4 1.9 %broadcast_multiply_fusion = f32[8,16,32,128]{3,2,1,0:T(8,128)S(1)} fusion(f32[8,16,32,128]{3,2,1,0:T(8,128)} %param.9, f32[16,32,128]{2,1,0:T(8,128)S(1)} %fusion.114), kind=kLoop, calls=%fused_computation.189 | loop fusion | flops 524288 | bytes 4456448 | tf_op jit(solution)/shard_map/mul | solution.py:144
  9.3 1.0 slice_select_fusion.2
  10.5 2.1 %collective-permute-start = (f32[8,2,32,128]{3,2,1,0:T(8,128)S(1)}, f32[8,2,32,128]{3,2,1,0:T(8,128)S(1)}, u32[]{:S(2)}, u32[]{:S(2)}) collective-permute-start(f32[8,2,32,128]{3,2,1,0:T(8,128)S(1)} %get-tuple-element.168), channel_id=1, source_target_pairs={{0,4},{4,0},{1,5},{5,1},{2,6},{6,2},{3,7},{7,3},{8,12},{12,8},{9,1... | collective-permute-start | bytes 786440 | tf_op jit(solution)/shard_map/ppermute | solution.py:24
  13.2 5.4 %collective-permute-done = f32[8,2,32,128]{3,2,1,0:T(8,128)S(1)} collective-permute-done((f32[8,2,32,128]{3,2,1,0:T(8,128)S(1)}, f32[8,2,32,128]{3,2,1,0:T(8,128)S(1)}, u32[]{:S(2)}, u32[]{:S(2)}) %collective-permute-start) | collective-permute-done | bytes 262176 | tf_op jit(solution)/shard_map/ppermute | solution.py:24
  18.6 5.7 %collective-permute-done.1 = f32[8,2,32,128]{3,2,1,0:T(8,128)S(1)} collective-permute-done((f32[8,2,32,128]{3,2,1,0:T(8,128)S(1)}, f32[8,2,32,128]{3,2,1,0:T(8,128)S(1)}, u32[]{:S(2)}, u32[]{:S(2)}) %collective-permute-start.1) | collective-permute-done | bytes 262176 | tf_op jit(solution)/shard_map/ppermute | solution.py:26
  24.4 1.3 collective-permute-start.2
  25.8 2.1 %collective-permute-start.3 = (f32[8,20,2,128]{3,2,1,0:T(2,128)S(1)}, f32[8,20,2,128]{3,2,1,0:T(2,128)}, u32[]{:S(2)}, u32[]{:S(2)}) collective-permute-start(f32[8,20,2,128]{3,2,1,0:T(2,128)S(1)} %get-tuple-element.163), channel_id=1, source_target_pairs={{1,0},{2,1},{3,2},{0,3},{5,4},{6,5},{7,6},{4,7},{9,8},{10,9},{11,1... | collective-permute-start | bytes 491528 | tf_op jit(solution)/shard_map/ppermute | solution.py:26
  28.5 2.4 %collective-permute-done.2 = f32[8,20,2,128]{3,2,1,0:T(2,128)S(1)} collective-permute-done((f32[8,20,2,128]{3,2,1,0:T(2,128)S(1)}, f32[8,20,2,128]{3,2,1,0:T(2,128)S(1)}, u32[]{:S(2)}, u32[]{:S(2)}) %collective-permute-start.2) | collective-permute-done | bytes 163872 | tf_op jit(solution)/shard_map/ppermute | solution.py:24
  31.6 3.3 %collective-permute-done.3 = f32[8,20,2,128]{3,2,1,0:T(2,128)} collective-permute-done((f32[8,20,2,128]{3,2,1,0:T(2,128)S(1)}, f32[8,20,2,128]{3,2,1,0:T(2,128)}, u32[]{:S(2)}, u32[]{:S(2)}) %collective-permute-start.3) | collective-permute-done | bytes 163872 | tf_op jit(solution)/shard_map/ppermute | solution.py:26
  34.9 2.3 %maximum_multiply_fusion = f32[8,20,36,128]{3,2,1,0:T(8,128)S(1)} fusion(f32[8,20,2,128]{3,2,1,0:T(2,128)} %collective-permute-done.3, f32[8,2,32,128]{3,2,1,0:T(8,128)} %copy-done.7, f32[8,16,32,128]{3,2,1,0:T(8,128)} %copy-done.2, f32[8,2,32,128]{3,2,1,0:T(8,128)} %copy-done.6, f32[8,20,2,128]{3,2,1,0:T(2,128)} %copy-done.8, f32[36]{0:T(128)S(1)} %and_convert_fusion), kind=kLoop, calls=%fused_computation.186 | loop fusion | flops 3686400 | bytes 5898384 | tf_op jit(solution)/shard_map/mul | solution.py:161
  37.2 4.3 %all-gather.7.cloned.1.call-done = f32[12,16,32,128]{3,2,1,0:T(8,128)} async-done(((f32[3,16,32,128]{3,2,1,0:T(8,128)}), f32[12,16,32,128]{3,2,1,0:T(8,128)}) %all-gather.7.cloned.1.call-update) | async-done | bytes 3145744 | tf_op jit(solution)/shard_map/all_gather | solution.py:35
  41.5 12.9 %conditional.3 = (f32[8,16,32,128]{3,2,1,0:T(8,128)S(1)}) conditional(s32[]{:T(128)} %convert_element_type.41, (f32[8,20,36,128]{3,2,1,0:T(8,128)S(1)}, f32[4,3,16,32,128]{4,3,2,1,0:T(8,128)}, f32[8,8]{1,0:T(8,128)S(1)}, f32[16,32,128]{2,1,0:T(8,128)S(1)}) %tuple.84, (f32[8,20,36,128]{3,2,1,0:T(8,128)S(1)}, f32[32]{0:T(128)S(1)}, ...), branch_computations={%region_0.2_spmd, %region_2.3_spmd} | conditional | flops 155859008 | bytes 44961804 | solution.py:156
  41.5 3.2 %reduce_sum.27 = f32[3,16,32,128]{3,2,1,0:T(8,128)} reduce(f32[4,3,16,32,128]{4,3,2,1,0:T(8,128)} %get-tuple-element.69, f32[]{:T(128)} %constant.79.clone), dimensions={0}, to_apply=%region_1.1 | reduce | flops 589824 | bytes 3932164 | tf_op jit(solution)/shard_map/reduce_sum | solution.py:35
  44.7 1.3 fusion.13
  46.0 1.7 %copy.15 = f32[8,20,36,128]{3,0,2,1:T(8,128)S(1)} copy(f32[8,20,36,128]{3,2,1,0:T(8,128)S(1)} %get-tuple-element.107) | data formatting | bytes 5898240 | tf_op jit(solution)/shard_map
  47.9 6.1 %fusion.8 = f32[8,16,32,128]{3,0,2,1:T(8,128)S(1)} fusion(f32[8,16,32,128]{3,0,2,1:T(8,128)S(1)} %slice.573, f32[8,20,36,128]{3,0,2,1:T(8,128)S(1)} %copy.15, f32[16,32,128]{2,1,0:T(8,128)S(1)} %get-tuple-element.71, f32[16,32,128]{2,1,0:T(8,128)S(1)} %get-tuple-element.121, f32[16,32,128]{2,1,0:T(8,128)S(1)} %get-tuple-element.122, ...), kind=kOutput, calls=%fused_computation.10 | convolution fusion | flops 72351744 | bytes 24645632 | tf_op jit(solution)/shard_map/cond/branch_0_fun/ij,jxyz->ixyz/dot_general | solution.py:109
  54.4 1.0 slice_select_fusion.1
  55.6 1.3 collective-permute-start.4
  57.1 3.8 %collective-permute-done.4 = f32[8,2,32,128]{3,2,1,0:T(8,128)S(1)} collective-permute-done((f32[8,2,32,128]{3,2,1,0:T(8,128)S(1)}, f32[8,2,32,128]{3,2,1,0:T(8,128)S(1)}, u32[]{:S(2)}, u32[]{:S(2)}) %collective-permute-start.4) | collective-permute-done | bytes 262176 | tf_op jit(solution)/shard_map/ppermute | solution.py:24
  60.9 3.1 %collective-permute-done.5 = f32[8,2,32,128]{3,2,1,0:T(8,128)S(1)} collective-permute-done((f32[8,2,32,128]{3,2,1,0:T(8,128)S(1)}, f32[8,2,32,128]{3,2,1,0:T(8,128)S(1)}, u32[]{:S(2)}, u32[]{:S(2)}) %collective-permute-start.5) | collective-permute-done | bytes 262176 | tf_op jit(solution)/shard_map/ppermute | solution.py:26
  64.1 1.3 collective-permute-start.6
  65.4 2.1 %collective-permute-start.7 = (f32[8,20,2,128]{3,2,1,0:T(2,128)S(1)}, f32[8,20,2,128]{3,2,1,0:T(2,128)S(1)}, u32[]{:S(2)}, u32[]{:S(2)}) collective-permute-start(f32[8,20,2,128]{3,2,1,0:T(2,128)S(1)} %get-tuple-element.161), channel_id=1, source_target_pairs={{1,0},{2,1},{3,2},{0,3},{5,4},{6,5},{7,6},{4,7},{9,8},{10,9},{11,1... | collective-permute-start | bytes 491528 | tf_op jit(solution)/shard_map/ppermute | solution.py:26
  67.4 2.8 %collective-permute-done.6 = f32[8,20,2,128]{3,2,1,0:T(2,128)S(1)} collective-permute-done((f32[8,20,2,128]{3,2,1,0:T(2,128)S(1)}, f32[8,20,2,128]{3,2,1,0:T(2,128)S(1)}, u32[]{:S(2)}, u32[]{:S(2)}) %collective-permute-start.6) | collective-permute-done | bytes 163872 | tf_op jit(solution)/shard_map/ppermute | solution.py:24
  70.2 1.5 collective-permute-done.7
  71.7 2.1 %maximum_multiply_fusion.1 = f32[8,20,36,128]{3,2,1,0:T(8,128)S(1)} fusion(f32[8,20,2,128]{3,2,1,0:T(2,128)S(1)} %collective-permute-done.7, f32[8,2,32,128]{3,2,1,0:T(8,128)S(1)} %collective-permute-done.5, f32[8,16,32,128]{3,2,1,0:T(8,128)} %copy-done.3, f32[8,2,32,128]{3,2,1,0:T(8,128)S(1)} %collective-permute-done.4, ...), kind=kLoop, calls=%fused_computation.187 | loop fusion | flops 3686400 | bytes 5898384 | tf_op jit(solution)/shard_map/mul | solution.py:161
  73.8 10.3 %all-gather.9.cloned.1.call-done = f32[12,16,32,128]{3,2,1,0:T(8,128)} async-done(((f32[3,16,32,128]{3,2,1,0:T(8,128)}), f32[12,16,32,128]{3,2,1,0:T(8,128)}) %all-gather.9.cloned.1.call-update) | async-done | bytes 3145744 | tf_op jit(solution)/shard_map/all_gather | solution.py:35
  84.1 12.9 %conditional.4 = (f32[8,16,32,128]{3,2,1,0:T(8,128)S(1)}) conditional(s32[]{:T(128)} %convert_element_type.41, (f32[8,20,36,128]{3,2,1,0:T(8,128)S(1)}, f32[4,3,16,32,128]{4,3,2,1,0:T(8,128)}, f32[8,8]{1,0:T(8,128)S(1)}, f32[16,32,128]{2,1,0:T(8,128)S(1)}) %tuple.86, (f32[8,20,36,128]{3,2,1,0:T(8,128)S(1)}, f32[32]{0:T(128)S(1)}, ...), branch_computations={%region_3.5_spmd, %region_5.6_spmd} | conditional | flops 155859008 | bytes 44961804 | solution.py:156
  84.2 3.2 %reduce_sum.28 = f32[3,16,32,128]{3,2,1,0:T(8,128)} reduce(f32[4,3,16,32,128]{4,3,2,1,0:T(8,128)} %get-tuple-element.77, f32[]{:T(128)} %constant.129.clone), dimensions={0}, to_apply=%region_4.4 | reduce | flops 589824 | bytes 3932164 | tf_op jit(solution)/shard_map/reduce_sum | solution.py:35
  87.3 1.3 fusion.51
  88.6 1.7 %copy.16 = f32[8,20,36,128]{3,0,2,1:T(8,128)S(1)} copy(f32[8,20,36,128]{3,2,1,0:T(8,128)S(1)} %get-tuple-element.111) | data formatting | bytes 5898240 | tf_op jit(solution)/shard_map
  90.5 6.1 %fusion.46 = f32[8,16,32,128]{3,0,2,1:T(8,128)S(1)} fusion(f32[8,16,32,128]{3,0,2,1:T(8,128)S(1)} %slice.596, f32[8,20,36,128]{3,0,2,1:T(8,128)S(1)} %copy.16, f32[16,32,128]{2,1,0:T(8,128)S(1)} %get-tuple-element.79, f32[16,32,128]{2,1,0:T(8,128)S(1)} %get-tuple-element.134, f32[16,32,128]{2,1,0:T(8,128)S(1)} %get-tuple-element.135, ...), kind=kOutput, calls=%fused_computation.72 | convolution fusion | flops 72351744 | bytes 24645632 | tf_op jit(solution)/shard_map/cond/branch_0_fun/ij,jxyz->ixyz/dot_general | solution.py:109
  97.1 1.0 slice_select_fusion
  98.2 1.3 collective-permute-start.8
  99.7 3.8 %collective-permute-done.8 = f32[8,2,32,128]{3,2,1,0:T(8,128)S(1)} collective-permute-done((f32[8,2,32,128]{3,2,1,0:T(8,128)S(1)}, f32[8,2,32,128]{3,2,1,0:T(8,128)S(1)}, u32[]{:S(2)}, u32[]{:S(2)}) %collective-permute-start.8) | collective-permute-done | bytes 262176 | tf_op jit(solution)/shard_map/ppermute | solution.py:24
  103.5 3.1 %collective-permute-done.9 = f32[8,2,32,128]{3,2,1,0:T(8,128)S(1)} collective-permute-done((f32[8,2,32,128]{3,2,1,0:T(8,128)S(1)}, f32[8,2,32,128]{3,2,1,0:T(8,128)S(1)}, u32[]{:S(2)}, u32[]{:S(2)}) %collective-permute-start.9) | collective-permute-done | bytes 262176 | tf_op jit(solution)/shard_map/ppermute | solution.py:26
  106.7 1.3 collective-permute-start.10
  108.0 2.1 %collective-permute-start.11 = (f32[8,20,2,128]{3,2,1,0:T(2,128)S(1)}, f32[8,20,2,128]{3,2,1,0:T(2,128)S(1)}, u32[]{:S(2)}, u32[]{:S(2)}) collective-permute-start(f32[8,20,2,128]{3,2,1,0:T(2,128)S(1)} %get-tuple-element.159), channel_id=1, source_target_pairs={{1,0},{2,1},{3,2},{0,3},{5,4},{6,5},{7,6},{4,7},{9,8},{10,9},{11,1... | collective-permute-start | bytes 491528 | tf_op jit(solution)/shard_map/ppermute | solution.py:26
  110.0 2.8 %collective-permute-done.10 = f32[8,20,2,128]{3,2,1,0:T(2,128)S(1)} collective-permute-done((f32[8,20,2,128]{3,2,1,0:T(2,128)S(1)}, f32[8,20,2,128]{3,2,1,0:T(2,128)S(1)}, u32[]{:S(2)}, u32[]{:S(2)}) %collective-permute-start.10) | collective-permute-done | bytes 163872 | tf_op jit(solution)/shard_map/ppermute | solution.py:24
  112.8 1.5 collective-permute-done.11
  114.3 2.1 %maximum_multiply_fusion.2 = f32[8,20,36,128]{3,2,1,0:T(8,128)S(1)} fusion(f32[8,20,2,128]{3,2,1,0:T(2,128)S(1)} %collective-permute-done.11, f32[8,2,32,128]{3,2,1,0:T(8,128)S(1)} %collective-permute-done.9, f32[8,16,32,128]{3,2,1,0:T(8,128)} %copy-done.4, f32[8,2,32,128]{3,2,1,0:T(8,128)S(1)} %collective-permute-done.8, ...), kind=kLoop, calls=%fused_computation.188 | loop fusion | flops 3686400 | bytes 5898384 | tf_op jit(solution)/shard_map/mul | solution.py:161
  116.4 10.4 %all-gather.11.cloned.1.call-done = f32[12,16,32,128]{3,2,1,0:T(8,128)} async-done(((f32[3,16,32,128]{3,2,1,0:T(8,128)}), f32[12,16,32,128]{3,2,1,0:T(8,128)}) %all-gather.11.cloned.1.call-update) | async-done | bytes 3145744 | tf_op jit(solution)/shard_map/all_gather | solution.py:35
  126.8 13.1 %conditional.5 = (f32[8,16,32,128]{3,2,1,0:T(8,128)S(1)}) conditional(s32[]{:T(128)} %convert_element_type.41, (f32[8,20,36,128]{3,2,1,0:T(8,128)S(1)}, f32[4,3,16,32,128]{4,3,2,1,0:T(8,128)}, f32[8,8]{1,0:T(8,128)S(1)}, f32[16,32,128]{2,1,0:T(8,128)S(1)}) %tuple.85, (f32[8,20,36,128]{3,2,1,0:T(8,128)S(1)}, f32[32]{0:T(128)S(1)}, ...), branch_computations={%region_6.8_spmd, %region_8.9_spmd} | conditional | flops 155859008 | bytes 44961804 | solution.py:156
  126.8 3.2 %reduce_sum.29 = f32[3,16,32,128]{3,2,1,0:T(8,128)} reduce(f32[4,3,16,32,128]{4,3,2,1,0:T(8,128)} %get-tuple-element.85, f32[]{:T(128)} %constant.163.clone), dimensions={0}, to_apply=%region_7.7 | reduce | flops 589824 | bytes 3932164 | tf_op jit(solution)/shard_map/reduce_sum | solution.py:35
  130.0 1.3 fusion.89
  131.3 1.7 %copy.17 = f32[8,20,36,128]{3,0,2,1:T(8,128)S(1)} copy(f32[8,20,36,128]{3,2,1,0:T(8,128)S(1)} %get-tuple-element.115) | data formatting | bytes 5898240 | tf_op jit(solution)/shard_map
  133.1 6.1 %fusion.84 = f32[8,16,32,128]{3,0,2,1:T(8,128)S(1)} fusion(f32[8,16,32,128]{3,0,2,1:T(8,128)S(1)} %slice.619, f32[8,20,36,128]{3,0,2,1:T(8,128)S(1)} %copy.17, f32[16,32,128]{2,1,0:T(8,128)S(1)} %get-tuple-element.87, f32[16,32,128]{2,1,0:T(8,128)S(1)} %get-tuple-element.147, f32[16,32,128]{2,1,0:T(8,128)S(1)} %get-tuple-element.148, ...), kind=kOutput, calls=%fused_computation.134 | convolution fusion | flops 72351744 | bytes 24645632 | tf_op jit(solution)/shard_map/cond/branch_0_fun/ij,jxyz->ixyz/dot_general | solution.py:109
  139.9 1.3 copy-done.5
  (44 shorter events, 5.5 us)
Async XLA Ops:
  6.5 6.6 %copy-start = (f32[3,8,8]{2,1,0:T(8,128)S(1)}, f32[3,8,8]{2,1,0:T(8,128)}, u32[]{:S(2)}) copy-start(f32[3,8,8]{2,1,0:T(8,128)} %param.11) | copy-start | bytes 2308
  6.5 35.0 %all-gather.7.cloned.1.call-start = ((), (), s32[]{:S(2)}) async-start(), calls=%async_computation | async-start | bytes 3932160 | tf_op jit(solution)/shard_map/all_gather | solution.py:35
  9.3 15.1 %copy-start.2 = (f32[8,16,32,128]{3,2,1,0:T(8,128)}, f32[8,16,32,128]{3,2,1,0:T(8,128)S(1)}, u32[]{:S(2)}) copy-start(f32[8,16,32,128]{3,2,1,0:T(8,128)S(1)} %broadcast_multiply_fusion) | copy-start | bytes 6291460
  10.4 73.8 %all-gather.9.cloned.1.call-start = ((), (), s32[]{:S(2)}) async-start(), calls=%async_computation.1 | async-start | bytes 3932160 | tf_op jit(solution)/shard_map/all_gather | solution.py:35
  10.5 8.1 %collective-permute-start = (f32[8,2,32,128]{3,2,1,0:T(8,128)S(1)}, f32[8,2,32,128]{3,2,1,0:T(8,128)S(1)}, u32[]{:S(2)}, u32[]{:S(2)}) collective-permute-start(f32[8,2,32,128]{3,2,1,0:T(8,128)S(1)} %get-tuple-element.168), channel_id=1, source_target_pairs={{0,4},{4,0},{1,5},{5,1},{2,6},{6,2},{3,7},{7,3},{8,12},{12,8},{9,1... | collective-permute-start | bytes 786440 | tf_op jit(solution)/shard_map/ppermute | solution.py:24
  12.6 11.7 %collective-permute-start.1 = (f32[8,2,32,128]{3,2,1,0:T(8,128)S(1)}, f32[8,2,32,128]{3,2,1,0:T(8,128)S(1)}, u32[]{:S(2)}, u32[]{:S(2)}) collective-permute-start(f32[8,2,32,128]{3,2,1,0:T(8,128)S(1)} %get-tuple-element.169), channel_id=1, source_target_pairs={{4,0},{0,4},{5,1},{1,5},{6,2},{2,6},{7,3},{3,7},{12,8},{8,12},{13,... | collective-permute-start | bytes 786440 | tf_op jit(solution)/shard_map/ppermute | solution.py:26
  18.6 12.4 %copy-start.6 = (f32[8,2,32,128]{3,2,1,0:T(8,128)}, f32[8,2,32,128]{3,2,1,0:T(8,128)S(1)}, u32[]{:S(2)}) copy-start(f32[8,2,32,128]{3,2,1,0:T(8,128)S(1)} %collective-permute-done) | copy-start | bytes 786436
  24.3 6.6 %copy-start.7 = (f32[8,2,32,128]{3,2,1,0:T(8,128)}, f32[8,2,32,128]{3,2,1,0:T(8,128)S(1)}, u32[]{:S(2)}) copy-start(f32[8,2,32,128]{3,2,1,0:T(8,128)S(1)} %collective-permute-done.1) | copy-start | bytes 786436
  24.4 6.5 %collective-permute-start.2 = (f32[8,20,2,128]{3,2,1,0:T(2,128)S(1)}, f32[8,20,2,128]{3,2,1,0:T(2,128)S(1)}, u32[]{:S(2)}, u32[]{:S(2)}) collective-permute-start(f32[8,20,2,128]{3,2,1,0:T(2,128)S(1)} %get-tuple-element.162), channel_id=1, source_target_pairs={{0,1},{1,2},{2,3},{3,0},{4,5},{5,6},{6,7},{7,4},{8,9},{9,10},{10,1... | collective-permute-start | bytes 491528 | tf_op jit(solution)/shard_map/ppermute | solution.py:24
  25.8 9.2 %collective-permute-start.3 = (f32[8,20,2,128]{3,2,1,0:T(2,128)S(1)}, f32[8,20,2,128]{3,2,1,0:T(2,128)}, u32[]{:S(2)}, u32[]{:S(2)}) collective-permute-start(f32[8,20,2,128]{3,2,1,0:T(2,128)S(1)} %get-tuple-element.163), channel_id=1, source_target_pairs={{1,0},{2,1},{3,2},{0,3},{5,4},{6,5},{7,6},{4,7},{9,8},{10,9},{11,1... | collective-permute-start | bytes 491528 | tf_op jit(solution)/shard_map/ppermute | solution.py:26
  28.5 13.0 %copy-start.9 = (f32[32]{0:T(128)S(1)}, f32[32]{0:T(128)}, u32[]{:S(2)}) copy-start(f32[32]{0:T(128)} %multiply_add_fusion.3) | copy-start | bytes 388
  30.9 0.7 copy-start.8
  54.4 9.7 %copy-start.3 = (f32[8,16,32,128]{3,2,1,0:T(8,128)}, f32[8,16,32,128]{3,2,1,0:T(8,128)S(1)}, u32[]{:S(2)}) copy-start(f32[8,16,32,128]{3,2,1,0:T(8,128)S(1)} %get-tuple-element.172) | copy-start | bytes 6291460
  55.5 71.3 %all-gather.11.cloned.1.call-start = ((), (), s32[]{:S(2)}) async-start(), calls=%async_computation.2 | async-start | bytes 3932160 | tf_op jit(solution)/shard_map/all_gather | solution.py:35
  55.6 5.3 %collective-permute-start.4 = (f32[8,2,32,128]{3,2,1,0:T(8,128)S(1)}, f32[8,2,32,128]{3,2,1,0:T(8,128)S(1)}, u32[]{:S(2)}, u32[]{:S(2)}) collective-permute-start(f32[8,2,32,128]{3,2,1,0:T(8,128)S(1)} %get-tuple-element.166), channel_id=1, source_target_pairs={{0,4},{4,0},{1,5},{5,1},{2,6},{6,2},{3,7},{7,3},{8,12},{12,8},{9,1... | collective-permute-start | bytes 786440 | tf_op jit(solution)/shard_map/ppermute | solution.py:24
  56.8 7.1 %collective-permute-start.5 = (f32[8,2,32,128]{3,2,1,0:T(8,128)S(1)}, f32[8,2,32,128]{3,2,1,0:T(8,128)S(1)}, u32[]{:S(2)}, u32[]{:S(2)}) collective-permute-start(f32[8,2,32,128]{3,2,1,0:T(8,128)S(1)} %get-tuple-element.167), channel_id=1, source_target_pairs={{4,0},{0,4},{5,1},{1,5},{6,2},{2,6},{7,3},{3,7},{12,8},{8,12},{13,... | collective-permute-start | bytes 786440 | tf_op jit(solution)/shard_map/ppermute | solution.py:26
  64.1 6.1 %collective-permute-start.6 = (f32[8,20,2,128]{3,2,1,0:T(2,128)S(1)}, f32[8,20,2,128]{3,2,1,0:T(2,128)S(1)}, u32[]{:S(2)}, u32[]{:S(2)}) collective-permute-start(f32[8,20,2,128]{3,2,1,0:T(2,128)S(1)} %get-tuple-element.160), channel_id=1, source_target_pairs={{0,1},{1,2},{2,3},{3,0},{4,5},{5,6},{6,7},{7,4},{8,9},{9,10},{10,1... | collective-permute-start | bytes 491528 | tf_op jit(solution)/shard_map/ppermute | solution.py:24
  65.4 6.3 %collective-permute-start.7 = (f32[8,20,2,128]{3,2,1,0:T(2,128)S(1)}, f32[8,20,2,128]{3,2,1,0:T(2,128)S(1)}, u32[]{:S(2)}, u32[]{:S(2)}) collective-permute-start(f32[8,20,2,128]{3,2,1,0:T(2,128)S(1)} %get-tuple-element.161), channel_id=1, source_target_pairs={{1,0},{2,1},{3,2},{0,3},{5,4},{6,5},{7,6},{4,7},{9,8},{10,9},{11,1... | collective-permute-start | bytes 491528 | tf_op jit(solution)/shard_map/ppermute | solution.py:26
  97.1 9.6 %copy-start.4 = (f32[8,16,32,128]{3,2,1,0:T(8,128)}, f32[8,16,32,128]{3,2,1,0:T(8,128)S(1)}, u32[]{:S(2)}) copy-start(f32[8,16,32,128]{3,2,1,0:T(8,128)S(1)} %get-tuple-element.173) | copy-start | bytes 6291460
  98.2 5.3 %collective-permute-start.8 = (f32[8,2,32,128]{3,2,1,0:T(8,128)S(1)}, f32[8,2,32,128]{3,2,1,0:T(8,128)S(1)}, u32[]{:S(2)}, u32[]{:S(2)}) collective-permute-start(f32[8,2,32,128]{3,2,1,0:T(8,128)S(1)} %get-tuple-element.164), channel_id=1, source_target_pairs={{0,4},{4,0},{1,5},{5,1},{2,6},{6,2},{3,7},{7,3},{8,12},{12,8},{9,1... | collective-permute-start | bytes 786440 | tf_op jit(solution)/shard_map/ppermute | solution.py:24
  99.4 7.1 %collective-permute-start.9 = (f32[8,2,32,128]{3,2,1,0:T(8,128)S(1)}, f32[8,2,32,128]{3,2,1,0:T(8,128)S(1)}, u32[]{:S(2)}, u32[]{:S(2)}) collective-permute-start(f32[8,2,32,128]{3,2,1,0:T(8,128)S(1)} %get-tuple-element.165), channel_id=1, source_target_pairs={{4,0},{0,4},{5,1},{1,5},{6,2},{2,6},{7,3},{3,7},{12,8},{8,12},{13,... | collective-permute-start | bytes 786440 | tf_op jit(solution)/shard_map/ppermute | solution.py:26
  106.7 6.1 %collective-permute-start.10 = (f32[8,20,2,128]{3,2,1,0:T(2,128)S(1)}, f32[8,20,2,128]{3,2,1,0:T(2,128)S(1)}, u32[]{:S(2)}, u32[]{:S(2)}) collective-permute-start(f32[8,20,2,128]{3,2,1,0:T(2,128)S(1)} %get-tuple-element.158), channel_id=1, source_target_pairs={{0,1},{1,2},{2,3},{3,0},{4,5},{5,6},{6,7},{7,4},{8,9},{9,10},{10,1... | collective-permute-start | bytes 491528 | tf_op jit(solution)/shard_map/ppermute | solution.py:24
  108.0 6.3 %collective-permute-start.11 = (f32[8,20,2,128]{3,2,1,0:T(2,128)S(1)}, f32[8,20,2,128]{3,2,1,0:T(2,128)S(1)}, u32[]{:S(2)}, u32[]{:S(2)}) collective-permute-start(f32[8,20,2,128]{3,2,1,0:T(2,128)S(1)} %get-tuple-element.159), channel_id=1, source_target_pairs={{1,0},{2,1},{3,2},{0,3},{5,4},{6,5},{7,6},{4,7},{9,8},{10,9},{11,1... | collective-permute-start | bytes 491528 | tf_op jit(solution)/shard_map/ppermute | solution.py:26
  139.9 1.3 copy-start.5
  141.2 0.7 copy-start.1
Sparse Core Ops, SparseCore 0:
  10.5 30.9 all-gather.6
  55.6 28.4 all-gather.8
  98.2 28.4 all-gather.10
